TPU v7x, 32 devices: a whole 2x2x4 slice. The times are simulated.
32 devices in a mesh: item: 2 (over x), lat: 4 (over y, core), pix: 4 (over z).
Axes of the slice: x: 2, y: 2, z: 4, core: 2. Of those that a mesh axis runs over, the one named last changes fastest.
Arguments:
- latents: bfloat16 [8, 512, 1024], P('item', ('lat', 'pix')), may hold values from -6 to 6
- pixels: bfloat16 [8, 32768, 261], P('item', ('lat', 'pix')), may hold values from -6 to 6
- size_ids: int32 [8], P('item'), may hold values from 0 to 2, as said below
- cross_gain: float32 [1024], replicated, may hold values from 0.25 to 1.75
- pixel_gain: float32 [261], replicated, may hold values from 0.25 to 1.75
- query_weight: bfloat16 [1024, 1024], replicated, may hold values from -0.1875 to 0.1875
- key_weight: bfloat16 [261, 1024], replicated, may hold values from -0.375 to 0.375
- value_weight: bfloat16 [261, 1024], replicated, may hold values from -0.375 to 0.375
- cross_output: bfloat16 [1024, 1024], replicated, may hold values from -9 to 9
- first_gain: float32 [1024], replicated, may hold values from 0.25 to 1.75
- first_up: bfloat16 [1024, 1024], replicated, may hold values from -0.1875 to 0.1875
- first_down: bfloat16 [1024, 1024], replicated, may hold values from -0.1875 to 0.1875
- self_gain: float32 [1024], replicated, may hold values from 0.25 to 1.75
- self_inputs: bfloat16 [1024, 3072], replicated, may hold values from -0.1875 to 0.1875
- self_output: bfloat16 [1024, 1024], replicated, may hold values from -2.5 to 2.5
- second_gain: float32 [1024], replicated, may hold values from 0.25 to 1.75
- second_up: bfloat16 [1024, 1024], replicated, may hold values from -0.1875 to 0.1875
- second_down: bfloat16 [1024, 1024], replicated, may hold values from -0.1875 to 0.1875
- cotangent: bfloat16 [8, 512, 1024], P('item', ('lat', 'pix')), may hold values from -6 to 6
Outputs:
- latents_out: bfloat16 [8, 512, 1024], P('item', ('lat', 'pix'))
- latent_grad: bfloat16 [8, 512, 1024], P('item', ('lat', 'pix'))
- pixel_grad: bfloat16 [8, 32768, 261], P('item', ('lat', 'pix'))
- query_grad: float32 [1024, 1024], P(('item', 'lat', 'pix'))
- cross_out_grad: float32 [1024, 1024], P(('item', 'lat', 'pix'))
- first_up_grad: float32 [1024, 1024], P(('item', 'lat', 'pix'))
- first_down_grad: float32 [1024, 1024], P(('item', 'lat', 'pix'))
- self_in_grad: float32 [1024, 3072], P(('item', 'lat', 'pix'))
- self_out_grad: float32 [1024, 1024], P(('item', 'lat', 'pix'))
- second_up_grad: float32 [1024, 1024], P(('item', 'lat', 'pix'))
- second_down_grad: float32 [1024, 1024], P(('item', 'lat', 'pix'))
- key_grad: float32 [261, 1024], replicated
- value_grad: float32 [261, 1024], replicated
- cross_gain_grad: float32 [1024], replicated
- pixel_gain_grad: float32 [261], replicated
- first_gain_grad: float32 [1024], replicated
- self_gain_grad: float32 [1024], replicated
- second_gain_grad: float32 [1024], replicated
Inputs may be any that keep to these rules, and one draw needn't show every extreme that they name: `size_ids`: each of the sizes 0, 1 and 2 is given to at least one image.
All inputs are finite; a program needn't handle non-finite values.
Results may differ from a plain program's by a relative error of at most 0.025.
Values may be sent and summed in bfloat16 or wider, within the bound.
No kernel may reach another device: no remote copies, remote signals or barrier semaphores. Data moves between devices by JAX's collectives and lax.ppermute only.
A program may use at most 256 MiB of HBM per device.

v0:
```python
import math
import jax
import jax.numpy as jnp
from jax import lax
from jax.sharding import PartitionSpec as P

HEADS = 8
epsilon = 1e-05


def norm_rows(inputs, gain):
    centred = inputs - jnp.mean(inputs, axis=-1, keepdims=True)
    inverse = lax.rsqrt(jnp.mean(centred * centred, axis=-1, keepdims=True) + epsilon)
    normed = centred * inverse
    return (normed * gain, normed, inverse)


def norm_back(upstream, normed, inverse, gain):
    scaled = upstream * gain
    first_mean = jnp.mean(scaled, axis=-1, keepdims=True)
    second_mean = jnp.mean(scaled * normed, axis=-1, keepdims=True)
    return inverse * (scaled - first_mean - normed * second_mean)


def activation(inputs):
    return jax.nn.gelu(inputs, approximate=True)


def forward_mat(left, right):
    return jnp.dot(left, right, preferred_element_type=jnp.float32)


def left_mat(left, right):
    return jnp.einsum("rk,rd->kd", left, right, preferred_element_type=jnp.float32)


def right_mat(left, right):
    return jnp.einsum("rd,kd->rk", left, right, preferred_element_type=jnp.float32)


def feed_forward(residual, gain, up_weight, down_weight):
    normed_full, normed, inverse = norm_rows(residual, gain)
    rounded_in = normed_full.astype(jnp.bfloat16)
    hidden = forward_mat(rounded_in, up_weight)
    active = activation(hidden).astype(jnp.bfloat16)
    return (
        residual + forward_mat(active, down_weight),
        (rounded_in, normed, inverse, hidden, active),
    )


def feed_back(upstream, kept, gain, up_weight, down_weight):
    rounded_in, normed, inverse, hidden, active = kept
    sent = upstream.astype(jnp.bfloat16)
    down_grad = left_mat(active, sent)
    unused, gelu_pull = jax.vjp(activation, hidden)
    hidden_grad = gelu_pull(right_mat(sent, down_weight))[0].astype(jnp.bfloat16)
    up_grad = left_mat(rounded_in, hidden_grad)
    normed_grad = right_mat(hidden_grad, up_weight)
    gain_grad = jnp.sum(normed_grad * normed, axis=0)
    return (upstream + norm_back(normed_grad, normed, inverse, gain), up_grad, down_grad, gain_grad)


def body(
    latents,
    pixels,
    size_ids,
    cross_gain,
    pixel_gain,
    query_weight,
    key_weight,
    value_weight,
    cross_output,
    first_gain,
    first_up,
    first_down,
    self_gain,
    self_inputs,
    self_output,
    second_gain,
    second_up,
    second_down,
    cotangent,
):
    images, lat_rows, width = latents.shape
    pix_rows = pixels.shape[1]
    head_dim = width // HEADS
    group = lax.axis_size(("lat", "pix"))
    block = lax.axis_index(("lat", "pix"))
    all_rows = lat_rows * group
    rows = images * lat_rows
    scale = 1.0 / math.sqrt(width)
    head_scale = 1.0 / math.sqrt(head_dim)
    factor = jnp.where(size_ids == 0, 25, jnp.where(size_ids == 1, 49, 81)).astype(jnp.int32)
    counts = pix_rows * group * factor // 81
    positions = block * pix_rows + jnp.arange(pix_rows, dtype=jnp.int32)
    valid = positions[None, :] < counts[:, None]
    residual_zero = latents.astype(jnp.float32).reshape(rows, width)
    normed_full, normed_one, inverse_one = norm_rows(residual_zero, cross_gain)
    rounded_one = normed_full.astype(jnp.bfloat16)
    query_own = (
        forward_mat(rounded_one, query_weight).astype(jnp.bfloat16).reshape(images, lat_rows, width)
    )
    query_all = lax.all_gather(query_own, ("lat", "pix"), axis=1, tiled=True)
    pixel_full, pixel_normed, pixel_inverse = norm_rows(pixels.astype(jnp.float32), pixel_gain)
    pixel_rounded = pixel_full.astype(jnp.bfloat16)
    pixel_keys = jnp.einsum(
        "ipc,cd->ipd", pixel_rounded, key_weight, preferred_element_type=jnp.float32
    ).astype(jnp.bfloat16)
    pixel_values = jnp.einsum(
        "ipc,cd->ipd", pixel_rounded, value_weight, preferred_element_type=jnp.float32
    ).astype(jnp.bfloat16)
    scores = (
        jnp.einsum("ild,ipd->ilp", query_all, pixel_keys, preferred_element_type=jnp.float32)
        * scale
    )
    powered = jnp.where(valid[:, None, :], jnp.exp(scores), 0.0)
    powered_low = powered.astype(jnp.bfloat16)
    totals = jnp.sum(powered, axis=2)
    numerator = jnp.einsum(
        "ilp,ipd->ild", powered_low, pixel_values, preferred_element_type=jnp.float32
    )
    numer_all, totals_all = (
        lax.psum(numerator.astype(jnp.bfloat16), ("lat", "pix")).astype(jnp.float32),
        lax.psum(totals.astype(jnp.bfloat16), ("lat", "pix")).astype(jnp.float32),
    )
    start = block * lat_rows
    numer_own = lax.dynamic_slice_in_dim(numer_all, start, lat_rows, 1)
    totals_own = lax.dynamic_slice_in_dim(totals_all, start, lat_rows, 1)
    attended = numer_own / totals_own[:, :, None]
    cross_mixed = attended.astype(jnp.bfloat16).reshape(rows, width)
    residual_one = residual_zero + forward_mat(cross_mixed, cross_output)
    residual_two, first_kept = feed_forward(residual_one, first_gain, first_up, first_down)
    normed_full, normed_three, inverse_three = norm_rows(residual_two, self_gain)
    rounded_three = normed_full.astype(jnp.bfloat16)
    projected = (
        forward_mat(rounded_three, self_inputs)
        .astype(jnp.bfloat16)
        .reshape(images, lat_rows, 3 * width)
    )
    pair_all = lax.all_gather(projected[:, :, width:], ("lat", "pix"), axis=1, tiled=True)
    self_query = projected[:, :, :width].reshape(images, lat_rows, HEADS, head_dim)
    self_keys = pair_all[:, :, :width].reshape(images, all_rows, HEADS, head_dim)
    self_values = pair_all[:, :, width:].reshape(images, all_rows, HEADS, head_dim)
    self_scores = (
        jnp.einsum("ilhe,imhe->ihlm", self_query, self_keys, preferred_element_type=jnp.float32)
        * head_scale
    )
    self_powered = jnp.exp(self_scores)
    self_low = self_powered.astype(jnp.bfloat16)
    self_totals = jnp.transpose(jnp.sum(self_powered, axis=3), (0, 2, 1))
    self_numerator = jnp.einsum(
        "ihlm,imhe->ilhe", self_low, self_values, preferred_element_type=jnp.float32
    )
    self_mixed = self_numerator / self_totals[..., None]
    self_rounded = self_mixed.astype(jnp.bfloat16).reshape(rows, width)
    residual_three = residual_two + forward_mat(self_rounded, self_output)
    output_rows, second_kept = feed_forward(residual_three, second_gain, second_up, second_down)
    latents_out = output_rows.astype(jnp.bfloat16).reshape(images, lat_rows, width)
    upstream = cotangent.astype(jnp.float32).reshape(rows, width)
    back_three, second_up_grad, second_down_grad, second_gain_grad = feed_back(
        upstream, second_kept, second_gain, second_up, second_down
    )
    sent_three = back_three.astype(jnp.bfloat16)
    self_out_grad = left_mat(self_rounded, sent_three)
    mixed_grad = (
        right_mat(sent_three, self_output)
        .astype(jnp.bfloat16)
        .reshape(images, lat_rows, HEADS, head_dim)
    )
    mixed_wide = mixed_grad.astype(jnp.float32)
    numer_grad = (mixed_wide / self_totals[..., None]).astype(jnp.bfloat16)
    total_grad = -jnp.sum(mixed_wide * self_mixed, axis=3) / self_totals
    power_grad = jnp.einsum(
        "ilhe,imhe->ihlm", numer_grad, self_values, preferred_element_type=jnp.float32
    )
    score_grad = (
        self_powered * (power_grad + jnp.transpose(total_grad, (0, 2, 1))[..., None])
    ).astype(jnp.bfloat16)
    query_part = (
        jnp.einsum("ihlm,imhe->ilhe", score_grad, self_keys, preferred_element_type=jnp.float32)
        * head_scale
    )
    key_part = (
        jnp.einsum("ihlm,ilhe->imhe", score_grad, self_query, preferred_element_type=jnp.float32)
        * head_scale
    )
    value_part = jnp.einsum(
        "ihlm,ilhe->imhe", self_low, numer_grad, preferred_element_type=jnp.float32
    )
    pair_grad = jnp.concatenate(
        [key_part.reshape(images, all_rows, width), value_part.reshape(images, all_rows, width)],
        axis=2,
    )
    pair_own = lax.psum_scatter(
        pair_grad.astype(jnp.bfloat16), ("lat", "pix"), scatter_dimension=1, tiled=True
    ).astype(jnp.float32)
    projected_grad = (
        jnp.concatenate([query_part.reshape(images, lat_rows, width), pair_own], axis=2)
        .astype(jnp.bfloat16)
        .reshape(rows, 3 * width)
    )
    self_in_grad = left_mat(rounded_three, projected_grad)
    normed_grad = right_mat(projected_grad, self_inputs)
    self_gain_grad = jnp.sum(normed_grad * normed_three, axis=0)
    back_two = back_three + norm_back(normed_grad, normed_three, inverse_three, self_gain)
    back_one, first_up_grad, first_down_grad, first_gain_grad = feed_back(
        back_two, first_kept, first_gain, first_up, first_down
    )
    sent_one = back_one.astype(jnp.bfloat16)
    cross_out_grad = left_mat(cross_mixed, sent_one)
    attended_grad = right_mat(sent_one, cross_output).astype(jnp.bfloat16).astype(jnp.float32)
    attended_grad = attended_grad.reshape(images, lat_rows, width)
    numer_own_grad = (attended_grad / totals_own[:, :, None]).astype(jnp.bfloat16)
    totals_own_grad = -jnp.sum(attended_grad * attended, axis=2) / totals_own
    numer_grad_all, totals_grad_all = (
        lax.all_gather(numer_own_grad, ("lat", "pix"), axis=1, tiled=True),
        lax.all_gather(
            totals_own_grad.astype(jnp.bfloat16), ("lat", "pix"), axis=1, tiled=True
        ).astype(totals_own_grad.dtype),
    )
    cross_power_grad = jnp.einsum(
        "ild,ipd->ilp", numer_grad_all, pixel_values, preferred_element_type=jnp.float32
    )
    cross_score_grad = (powered * (cross_power_grad + totals_grad_all[:, :, None])).astype(
        jnp.bfloat16
    )
    query_part_cross = (
        jnp.einsum("ilp,ipd->ild", cross_score_grad, pixel_keys, preferred_element_type=jnp.float32)
        * scale
    )
    query_rows_grad = lax.psum_scatter(
        query_part_cross.astype(jnp.bfloat16), ("lat", "pix"), scatter_dimension=1, tiled=True
    ).astype(jnp.float32)
    query_rows_grad = query_rows_grad.astype(jnp.bfloat16).reshape(rows, width)
    key_rows_grad = (
        jnp.einsum("ilp,ild->ipd", cross_score_grad, query_all, preferred_element_type=jnp.float32)
        * scale
    ).astype(jnp.bfloat16)
    value_rows_grad = jnp.einsum(
        "ilp,ild->ipd", powered_low, numer_grad_all, preferred_element_type=jnp.float32
    ).astype(jnp.bfloat16)
    pixel_normed_grad = jnp.einsum(
        "ipd,cd->ipc", key_rows_grad, key_weight, preferred_element_type=jnp.float32
    ) + jnp.einsum("ipd,cd->ipc", value_rows_grad, value_weight, preferred_element_type=jnp.float32)
    key_grad = jnp.einsum(
        "ipc,ipd->cd", pixel_rounded, key_rows_grad, preferred_element_type=jnp.float32
    )
    value_grad = jnp.einsum(
        "ipc,ipd->cd", pixel_rounded, value_rows_grad, preferred_element_type=jnp.float32
    )
    pixel_gain_grad = jnp.sum(pixel_normed_grad * pixel_normed, axis=(0, 1))
    pixel_grad = norm_back(pixel_normed_grad, pixel_normed, pixel_inverse, pixel_gain).astype(
        jnp.bfloat16
    )
    query_grad = left_mat(rounded_one, query_rows_grad)
    normed_one_grad = right_mat(query_rows_grad, query_weight)
    cross_gain_grad = jnp.sum(normed_one_grad * normed_one, axis=0)
    latent_grad = back_one + norm_back(normed_one_grad, normed_one, inverse_one, cross_gain)
    latent_grad = latent_grad.astype(jnp.bfloat16).reshape(images, lat_rows, width)
    (
        query_grad,
        cross_out_grad,
        first_up_grad,
        first_down_grad,
        self_in_grad,
        self_out_grad,
        second_up_grad,
        second_down_grad,
    ) = (
        lax.psum_scatter(query_grad, ("item", "lat", "pix"), scatter_dimension=0, tiled=True),
        lax.psum_scatter(cross_out_grad, ("item", "lat", "pix"), scatter_dimension=0, tiled=True),
        lax.psum_scatter(first_up_grad, ("item", "lat", "pix"), scatter_dimension=0, tiled=True),
        lax.psum_scatter(first_down_grad, ("item", "lat", "pix"), scatter_dimension=0, tiled=True),
        lax.psum_scatter(self_in_grad, ("item", "lat", "pix"), scatter_dimension=0, tiled=True),
        lax.psum_scatter(self_out_grad, ("item", "lat", "pix"), scatter_dimension=0, tiled=True),
        lax.psum_scatter(second_up_grad, ("item", "lat", "pix"), scatter_dimension=0, tiled=True),
        lax.psum_scatter(second_down_grad, ("item", "lat", "pix"), scatter_dimension=0, tiled=True),
    )
    (
        key_grad,
        value_grad,
        cross_gain_grad,
        pixel_gain_grad,
        first_gain_grad,
        self_gain_grad,
        second_gain_grad,
    ) = lax.psum(
        (
            key_grad,
            value_grad,
            cross_gain_grad,
            pixel_gain_grad,
            first_gain_grad,
            self_gain_grad,
            second_gain_grad,
        ),
        ("item", "lat", "pix"),
    )
    return (
        latents_out,
        latent_grad,
        pixel_grad,
        query_grad,
        cross_out_grad,
        first_up_grad,
        first_down_grad,
        self_in_grad,
        self_out_grad,
        second_up_grad,
        second_down_grad,
        key_grad,
        value_grad,
        cross_gain_grad,
        pixel_gain_grad,
        first_gain_grad,
        self_gain_grad,
        second_gain_grad,
    )


def solution(mesh):
    in_specs = (
        P("item", ("lat", "pix"), None),
        P("item", ("lat", "pix"), None),
        P("item"),
        P(),
        P(),
        P(),
        P(),
        P(),
        P(),
        P(),
        P(),
        P(),
        P(),
        P(),
        P(),
        P(),
        P(),
        P(),
        P("item", ("lat", "pix"), None),
    )
    out_specs = (
        P("item", ("lat", "pix"), None),
        P("item", ("lat", "pix"), None),
        P("item", ("lat", "pix"), None),
        P(("item", "lat", "pix"), None),
        P(("item", "lat", "pix"), None),
        P(("item", "lat", "pix"), None),
        P(("item", "lat", "pix"), None),
        P(("item", "lat", "pix"), None),
        P(("item", "lat", "pix"), None),
        P(("item", "lat", "pix"), None),
        P(("item", "lat", "pix"), None),
        P(),
        P(),
        P(),
        P(),
        P(),
        P(),
        P(),
    )
    return jax.shard_map(body, mesh=mesh, in_specs=in_specs, out_specs=out_specs, check_vma=False)
```

profile of v0, /device:TPU:0, one launch (start us, length us, event | category | flops | bytes accessed | tf_op | source)
XLA Modules:
  0.0 2006.8 jit_solution(15135687993326305070)
XLA Ops:
  14.7 5.0 convert_reduce_fusion
  22.3 20.6 %convolution_convert_fusion.1 = bf16[4,2048,1024]{2,1,0:T(8,128)(2,1)} fusion(bf16[261,1024]{1,0:T(8,128)(2,1)S(1)} %copy-done.60, f32[261]{0:T(512)S(1)} %copy-done.56, f32[4,2048]{1,0:T(4,128)S(1)} %add_rsqrt_fusion, f32[4,2048]{1,0:T(4,128)S(1)} %broadcast_multiply_fusion.2, bf16[4,2048,261]{1,0,2:T(4,128)(2,1)S(1)} %copy-done.3), kind=kOutput, calls=%fused_computation.4 | convolution fusion | flops 4397932544 | bytes 21654548 | tf_op jit(solution)/shard_map/ipc,cd->ipd/dot_general | solution.py:110
  42.9 20.6 %convolution_convert_fusion.2 = bf16[4,2048,1024]{2,1,0:T(8,128)(2,1)} fusion(bf16[261,1024]{1,0:T(8,128)(2,1)S(1)} %copy-done.58, f32[261]{0:T(512)S(1)} %copy-done.56, f32[4,2048]{1,0:T(4,128)S(1)} %add_rsqrt_fusion, f32[4,2048]{1,0:T(4,128)S(1)} %broadcast_multiply_fusion.2, bf16[4,2048,261]{1,0,2:T(4,128)(2,1)S(1)} %copy-done.3), kind=kOutput, calls=%fused_computation.5 | convolution fusion | flops 4397932544 | bytes 21654548 | tf_op jit(solution)/shard_map/ipc,cd->ipd/dot_general | solution.py:107
  67.1 18.3 fusion
  85.4 18.5 convolution_convert_fusion.5
  104.0 32.8 %psum.64 = bf16[4,512]{1,0:T(4,128)(2,1)S(1)} all-reduce(bf16[4,512]{1,0:T(4,128)(2,1)S(1)} %get-tuple-element.116), channel_id=1, replica_groups=mesh['item'=2,'lat'=4,'pix'=4] {'lat','pix'}, use_global_device_ids=true, to_apply=%region_6.7 | all-reduce | flops 2048 | bytes 8192 | tf_op jit(solution)/shard_map/psum | solution.py:125
  136.9 78.2 %all-reduce.5.cloned.1.call-done = bf16[4,512,1024]{2,1,0:T(8,128)(2,1)} async-done(((bf16[4,512,1024]{2,1,0:T(8,128)(2,1)}), bf16[4,512,1024]{2,1,0:T(8,128)(2,1)}) %all-reduce.5.cloned.1.call-update) | async-done | bytes 4194320 | tf_op jit(solution)/shard_map/psum | solution.py:124
  220.3 3.9 convolution_convert_fusion.3
  229.7 70.3 %all-gather.7.cloned.1.call-done = bf16[4,512,2048]{2,0,1:T(4,128)(2,1)} async-done(((bf16[4,32,2048]{2,0,1:T(4,128)(2,1)}), bf16[4,512,2048]{2,0,1:T(4,128)(2,1)}) %all-gather.7.cloned.1.call-update) | async-done | bytes 8388624 | tf_op jit(solution)/shard_map/all_gather | solution.py:141
  299.9 8.3 fusion.91
  308.2 7.5 copy.107
  315.7 4.4 fusion.94
  320.1 7.5 copy.106
  327.6 4.5 fusion.95
  337.3 4.3 convolution_convert_fusion.4
  342.6 6.2 copy.94
  348.8 4.3 multiply_convert_fusion.3
  353.1 6.3 copy.93
  359.4 8.2 pad_maximum_fusion
  367.8 3.7 fusion.22
  371.7 98.1 %reduce-scatter.11.cloned.1.call-done = bf16[4,32,2048]{2,1,0:T(8,128)(2,1)} async-done(((bf16[4,512,2048]{2,1,0:T(8,128)(2,1)}), bf16[4,32,2048]{2,1,0:T(8,128)(2,1)}) %reduce-scatter.11.cloned.1.call-update) | async-done | bytes 524304 | tf_op jit(solution)/shard_map/reduce_scatter | solution.py:195
  469.8 5.4 multiply_reduce_fusion.2
  481.9 31.2 %all-gather = bf16[16,32,4]{1,2,0:T(4,128)(2,1)S(1)} all-gather(bf16[1,32,4]{1,2,0:T(4,128)(2,1)S(1)} %fusion.74), channel_id=1, replica_groups=mesh['item'=2,'lat'=4,'pix'=4] {'lat','pix'}, dimensions={0}, use_global_device_ids=true | all-gather | bytes 4352 | tf_op jit(solution)/shard_map/all_gather | solution.py:218
  513.2 19.0 all-gather.9.cloned.1.call-done
  532.2 16.2 multiply_convert_fusion.1
  551.6 13.7 multiply_convert_fusion.2
  572.5 3.9 fusion.82
  585.1 13.2 convolution_convert_fusion
  598.3 5.7 copy-done.63
  604.0 11.7 convolution_bitcast_fusion.1
  615.7 16.0 multiply_convert_fusion
  631.7 16.3 convolution_bitcast_fusion.2
  648.2 6.4 fusion.47
  655.5 3.8 convolution_bitcast_fusion
  662.2 19.6 fusion.25
  681.9 17.8 fusion.13
  699.7 6.4 fusion.12
  706.2 5.3 copy.98
  712.6 41.0 %all-reduce = (f32[1024]{0:T(1024)}, f32[261]{0:T(512)}, f32[1024]{0:T(1024)}, f32[1024]{0:T(1024)}, f32[1024]{0:T(1024)}) all-reduce(f32[1024]{0:T(1024)S(1)} %get-tuple-element.99, f32[261]{0:T(512)S(1)} %get-tuple-element.90, f32[1024]{0:T(1024)S(1)} %get-tuple-element.97, ...), channel_id=1, replica_groups=mesh['item'=2,'lat'=4,'pix'=4] {'item','lat','pix'}, use_global_device_ids=true, to_apply=%region_39.40 | all-reduce | flops 4357 | bytes 34856 | tf_op jit(solution)/shard_map/psum | solution.py:288
  754.5 34.3 %reduce-scatter.27.cloned.1.call-done = f32[32,1024]{1,0:T(8,128)} async-done(((f32[1024,1024]{1,0:T(8,128)}), f32[32,1024]{1,0:T(8,128)}) %reduce-scatter.27.cloned.1.call-update) | async-done | bytes 131088 | tf_op jit(solution)/shard_map/reduce_scatter | solution.py:277
  788.8 151.1 %reduce-scatter.25.cloned.1.call-done = f32[32,1024]{1,0:T(8,128)} async-done(((f32[1024,1024]{1,0:T(8,128)}), f32[32,1024]{1,0:T(8,128)}) %reduce-scatter.25.cloned.1.call-update) | async-done | bytes 131088 | tf_op jit(solution)/shard_map/reduce_scatter | solution.py:276
  939.9 151.1 %reduce-scatter.29.cloned.1.call-done = f32[32,1024]{1,0:T(8,128)} async-done(((f32[1024,1024]{1,0:T(8,128)}), f32[32,1024]{1,0:T(8,128)}) %reduce-scatter.29.cloned.1.call-update) | async-done | bytes 131088 | tf_op jit(solution)/shard_map/reduce_scatter | solution.py:278
  1091.0 150.5 %reduce-scatter.21.cloned.1.call-done = f32[32,1024]{1,0:T(8,128)} async-done(((f32[1024,1024]{1,0:T(8,128)}), f32[32,1024]{1,0:T(8,128)}) %reduce-scatter.21.cloned.1.call-update) | async-done | bytes 131088 | tf_op jit(solution)/shard_map/reduce_scatter | solution.py:274
  1241.5 150.9 %reduce-scatter.19.cloned.1.call-done = f32[32,1024]{1,0:T(8,128)} async-done(((f32[1024,1024]{1,0:T(8,128)}), f32[32,1024]{1,0:T(8,128)}) %reduce-scatter.19.cloned.1.call-update) | async-done | bytes 131088 | tf_op jit(solution)/shard_map/reduce_scatter | solution.py:273
  1392.4 151.4 %reduce-scatter.17.cloned.1.call-done = f32[32,1024]{1,0:T(8,128)} async-done(((f32[1024,1024]{1,0:T(8,128)}), f32[32,1024]{1,0:T(8,128)}) %reduce-scatter.17.cloned.1.call-update) | async-done | bytes 131088 | tf_op jit(solution)/shard_map/reduce_scatter | solution.py:272
  1543.8 140.2 %all-reduce.7.cloned.1.call-done = (f32[261,1024]{1,0:T(8,128)}, f32[261,1024]{1,0:T(8,128)}) async-done(((f32[261,1024]{1,0:T(8,128)}, f32[261,1024]{1,0:T(8,128)}), (f32[261,1024]{1,0:T(8,128)}, f32[261,1024]{1,0:T(8,128)})) %all-reduce.7.cloned.1.call-update) | async-done | bytes 2138128 | tf_op jit(solution)/shard_map/psum | solution.py:288
  1684.0 160.5 %reduce-scatter.23.cloned.1.call-done = f32[32,3072]{1,0:T(8,128)} async-done(((f32[1024,3072]{1,0:T(8,128)}), f32[32,3072]{1,0:T(8,128)}) %reduce-scatter.23.cloned.1.call-update) | async-done | bytes 393232 | tf_op jit(solution)/shard_map/reduce_scatter | solution.py:275
  1844.5 150.6 %reduce-scatter.15.cloned.1.call-done = f32[32,1024]{1,0:T(8,128)} async-done(((f32[1024,1024]{1,0:T(8,128)}), f32[32,1024]{1,0:T(8,128)}) %reduce-scatter.15.cloned.1.call-update) | async-done | bytes 131088 | tf_op jit(solution)/shard_map/reduce_scatter | solution.py:271
  (237 shorter events, 66.7 us)
Async XLA Ops:
  7.2 325.8 %copy-start = (bf16[1024,1024]{1,0:T(8,128)(2,1)S(1)}, bf16[1024,1024]{1,0:T(8,128)(2,1)}, u32[]{:S(2)}) copy-start(bf16[1024,1024]{1,0:T(8,128)(2,1)} %param.35) | copy-start | bytes 6291460
  7.2 59.9 %all-gather.5.cloned.1.call-start = ((), (), s32[]{:S(2)}) async-start(), calls=%async_computation.10 | async-start | bytes 4456448 | tf_op jit(solution)/shard_map/all_gather | solution.py:104
  8.5 13.7 copy-start.46
  8.6 13.6 copy-start.52
  9.7 12.4 copy-start.50
  9.8 12.4 copy-start.54
  13.8 201.3 %all-reduce.5.cloned.1.call-start = ((), (), s32[]{:S(2)}) async-start(), calls=%async_computation.11 | async-start | bytes 8388608 | tf_op jit(solution)/shard_map/psum | solution.py:124
  13.8 5.9 copy-start.3
  14.7 7.5 copy-start.56
  14.7 7.5 copy-start.60
  19.8 23.1 %copy-start.39 = (f32[4,2048]{1,0:T(4,128)}, f32[4,2048]{1,0:T(4,128)S(1)}, u32[]{:S(2)}) copy-start(f32[4,2048]{1,0:T(4,128)S(1)} %broadcast_multiply_fusion.2) | copy-start | bytes 98308
  22.2 20.6 %copy-start.42 = (f32[4,2048]{1,0:T(4,128)}, f32[4,2048]{1,0:T(4,128)S(1)}, u32[]{:S(2)}) copy-start(f32[4,2048]{1,0:T(4,128)S(1)} %add_rsqrt_fusion) | copy-start | bytes 98308
  22.3 20.6 %copy-start.58 = (bf16[261,1024]{1,0:T(8,128)(2,1)S(1)}, bf16[261,1024]{1,0:T(8,128)(2,1)}, u32[]{:S(2)}) copy-start(bf16[261,1024]{1,0:T(8,128)(2,1)} %param.25) | copy-start | bytes 1603588
  103.9 112.5 %copy-start.15 = (bf16[4,32,1024]{2,1,0:T(8,128)(2,1)S(1)}, bf16[4,32,1024]{2,1,0:T(8,128)(2,1)}, u32[]{:S(2)}) copy-start(bf16[4,32,1024]{2,1,0:T(8,128)(2,1)} %param.19) | copy-start | bytes 786436
  103.9 115.0 %copy-start.44 = (f32[1024]{0:T(1024)S(1)}, f32[1024]{0:T(1024)}, u32[]{:S(2)}) copy-start(f32[1024]{0:T(1024)} %param.28) | copy-start | bytes 12292
  103.9 196.0 %all-gather.7.cloned.1.call-start = ((), (), s32[]{:S(2)}) async-start(), calls=%async_computation.12 | async-start | bytes 8912896 | tf_op jit(solution)/shard_map/all_gather | solution.py:141
  220.3 6.1 copy-start.25
  226.3 243.4 %reduce-scatter.11.cloned.1.call-start = ((), (), s32[]{:S(2)}) async-start(), calls=%async_computation.13 | async-start | bytes 8912896 | tf_op jit(solution)/shard_map/reduce_scatter | solution.py:195
  327.6 5.5 copy-start.38
  327.6 5.5 copy-start.45
  367.6 164.6 %all-gather.9.cloned.1.call-start = ((), (), s32[]{:S(2)}) async-start(), calls=%async_computation.14 | async-start | bytes 4456448 | tf_op jit(solution)/shard_map/all_gather | solution.py:217
  371.7 98.1 %copy-start.35 = (bf16[16,8,8,128]{3,1,2,0:T(8,128)(2,1)}, bf16[16,8,8,128]{3,1,2,0:T(8,128)(2,1)S(1)}, u32[]{:S(2)}) copy-start(bf16[16,8,8,128]{3,1,2,0:T(8,128)(2,1)S(1)} %copy.148) | copy-start | bytes 786436
  469.8 6.9 copy-start.21
  469.8 6.9 copy-start.29
  479.0 103.3 %copy-start.7 = (f32[128,1024]{1,0:T(8,128)}, f32[128,1024]{1,0:T(8,128)S(1)}, u32[]{:S(2)}) copy-start(f32[128,1024]{1,0:T(8,128)S(1)} %multiply_add_fusion) | copy-start | bytes 1572868
  481.8 172.9 %reduce-scatter.13.cloned.1.call-start = ((), (), s32[]{:S(2)}) async-start(), calls=%async_computation.15 | async-start | bytes 4456448 | tf_op jit(solution)/shard_map/reduce_scatter | solution.py:232
  565.3 223.4 %reduce-scatter.27.cloned.1.call-start = ((), (), s32[]{:S(2)}) async-start(), calls=%async_computation.22 | async-start | bytes 4325376 | tf_op jit(solution)/shard_map/reduce_scatter | solution.py:277
  569.2 370.7 %reduce-scatter.25.cloned.1.call-start = ((), (), s32[]{:S(2)}) async-start(), calls=%async_computation.21 | async-start | bytes 4325376 | tf_op jit(solution)/shard_map/reduce_scatter | solution.py:276
  572.5 518.5 %reduce-scatter.29.cloned.1.call-start = ((), (), s32[]{:S(2)}) async-start(), calls=%async_computation.23 | async-start | bytes 4325376 | tf_op jit(solution)/shard_map/reduce_scatter | solution.py:278
  576.5 665.0 %reduce-scatter.21.cloned.1.call-start = ((), (), s32[]{:S(2)}) async-start(), calls=%async_computation.19 | async-start | bytes 4325376 | tf_op jit(solution)/shard_map/reduce_scatter | solution.py:274
  579.4 813.0 %reduce-scatter.19.cloned.1.call-start = ((), (), s32[]{:S(2)}) async-start(), calls=%async_computation.18 | async-start | bytes 4325376 | tf_op jit(solution)/shard_map/reduce_scatter | solution.py:273
  582.2 961.6 %reduce-scatter.17.cloned.1.call-start = ((), (), s32[]{:S(2)}) async-start(), calls=%async_computation.17 | async-start | bytes 4325376 | tf_op jit(solution)/shard_map/reduce_scatter | solution.py:272
  585.0 19.0 copy-start.40
  585.0 19.0 copy-start.43
  585.1 19.0 copy-start.57
  585.1 1098.9 %all-reduce.7.cloned.1.call-start = ((), (), s32[]{:S(2)}) async-start(), calls=%async_computation.24 | async-start | bytes 4325376 | tf_op jit(solution)/shard_map/psum | solution.py:288
  598.3 5.7 copy-start.63
  631.7 16.4 copy-start.36
  631.7 16.4 copy-start.37
  648.1 1196.4 %reduce-scatter.23.cloned.1.call-start = ((), (), s32[]{:S(2)}) async-start(), calls=%async_computation.20 | async-start | bytes 12976128 | tf_op jit(solution)/shard_map/reduce_scatter | solution.py:275
  654.6 1340.6 %reduce-scatter.15.cloned.1.call-start = ((), (), s32[]{:S(2)}) async-start(), calls=%async_computation.16 | async-start | bytes 4325376 | tf_op jit(solution)/shard_map/reduce_scatter | solution.py:271
  659.3 22.6 %slice-start = ((s8[4276224]{0:T(1024)(128)(4,1)}), s8[81920]{0:T(1024)(128)(4,1)S(1)}, s32[]{:S(2)}) async-start(s8[4276224]{0:T(1024)(128)(4,1)} %bitcast.147), calls=%async_computation.25 | async-start | bytes 163840
  662.2 19.6 slice-start.1
  662.2 19.6 copy-start.61
  706.2 5.4 copy-start.27
  706.2 6.4 copy-start.49
  706.2 47.3 %copy-start.8 = (f32[128,1024]{1,0:T(8,128)S(1)}, f32[128,1024]{1,0:T(8,128)}, u32[]{:S(2)}) copy-start(f32[128,1024]{1,0:T(8,128)} %copy-done.7) | copy-start | bytes 1572868
  711.6 1288.3 %copy-start.1 = (bf16[1024,1024]{1,0:T(8,128)(2,1)S(1)}, bf16[1024,1024]{1,0:T(8,128)(2,1)}, u32[]{:S(2)}) copy-start(bf16[1024,1024]{1,0:T(8,128)(2,1)} %param.35) | copy-start | bytes 6291460
  (34 other events, 97.7 us)
Sparse Core Ops, SparseCore 0:
  13.9 53.1 all-gather.4
  104.0 111.0 all-reduce.4
  226.5 73.4 all-gather.6
  367.7 102.0 reduce-scatter.10
  481.9 50.2 all-gather.8
  565.4 71.2 reduce-scatter.12
  639.6 149.1 reduce-scatter.26
  791.6 148.2 reduce-scatter.24
  942.7 148.2 reduce-scatter.28
  1093.7 147.7 reduce-scatter.20
  1244.4 147.9 reduce-scatter.18
  1395.1 148.6 reduce-scatter.16
  1550.1 133.8 all-reduce.6
  1690.5 154.0 reduce-scatter.22
  1847.2 147.8 reduce-scatter.14
where the time goes:
time: 2010 us
  waiting for transfers between devices  1510 us (75%)
  matrix products  282 us (14%)
  blocking collectives  105 us (5%)
  local copies, waits for them, and re-layouts  59.6 us (3%)
  other arithmetic  33.4 us (2%)
    reduce_scatter x1, waiting for transfers between devices, body(): lax.psum_scatter(self_in_grad, ('item', 'lat', 'pix'), scatter_dimension=...  161 us
    reduce_scatter x1, waiting for transfers between devices, body(): lax.psum_scatter(cross_out_grad, ('item', 'lat', 'pix'), scatter_dimensio...  151 us
    reduce_scatter x1, waiting for transfers between devices, body(): lax.psum_scatter(second_down_grad, ('item', 'lat', 'pix'), scatter_dimens...  151 us
    reduce_scatter x1, waiting for transfers between devices, body(): lax.psum_scatter(self_out_grad, ('item', 'lat', 'pix'), scatter_dimension...  151 us
    reduce_scatter x1, waiting for transfers between devices, body(): lax.psum_scatter(first_up_grad, ('item', 'lat', 'pix'), scatter_dimension...  151 us
    reduce_scatter x1, waiting for transfers between devices, body(): lax.psum_scatter(query_grad, ('item', 'lat', 'pix'), scatter_dimension=0,...  151 us
    reduce_scatter x1, waiting for transfers between devices, body(): lax.psum_scatter(first_down_grad, ('item', 'lat', 'pix'), scatter_dimensi...  151 us
    psum x1, waiting for transfers between devices, body(): lax.psum((key_grad, value_grad, cross_gain_grad, pixel_gain_grad, first_g...  140 us
  transfers between devices with their start and end apart: 15, of which 14 were waited for; matrix products, arithmetic and copies ran while one was open for 10% of the time, Pallas kernels for 0%

commit v1 on v0

--- a/solution.py
+++ b/solution.py
@@ -121,7 +121,9 @@
         "ilp,ipd->ild", powered_low, pixel_values, preferred_element_type=jnp.float32
     )
     numer_all, totals_all = (
-        lax.psum(numerator.astype(jnp.bfloat16), ("lat", "pix")).astype(jnp.float32),
+        jnp.sum(lax.all_gather(numerator.astype(jnp.bfloat16), ("lat", "pix")), axis=0).astype(
+            jnp.float32
+        ),
         lax.psum(totals.astype(jnp.bfloat16), ("lat", "pix")).astype(jnp.float32),
     )
     start = block * lat_rows

time: 2010 us -> 2270 us (1.13)
  waiting for transfers between devices: 1510 us -> 1740 us
  other arithmetic: 33.4 us -> 57.3 us
    all_gather x0 -> x1, waiting for transfers between devices: none -> 314 us  [body(): lax.all_gather(numerator.astype(jnp.bfloat16), ('lat', 'pix'))]
    psum x1 -> x0, waiting for transfers between devices: 78.2 us -> none  [body(): lax.psum(numerator.astype(jnp.bfloat16), ('lat', 'pix')).astype(jnp.float32)]
    reduce_sum x0 -> x1, other arithmetic: none -> 23.8 us  [body(): jnp.sum(lax.all_gather(numerator.astype(jnp.bfloat16), ('lat', 'pix')), a...]
  transfers between devices with their start and end apart: 15 -> 15, of which waited for: 14 -> 14; matrix products, arithmetic and copies ran while one was open for 10% -> 9% of each run, Pallas kernels for 0% -> 0%
where the time goes in v1:
time: 2270 us; the launch traced here: 2260 us
  waiting for transfers between devices  1740 us (77%)
  matrix products  280 us (12%)
  blocking collectives  105 us (5%)
  local copies, waits for them, and re-layouts  60.9 us (3%)
  other arithmetic  57.3 us (3%)
    all_gather x1, waiting for transfers between devices, body(): lax.all_gather(numerator.astype(jnp.bfloat16), ('lat', 'pix'))  314 us
    reduce_scatter x1, waiting for transfers between devices, body(): lax.psum_scatter(self_in_grad, ('item', 'lat', 'pix'), scatter_dimension=...  161 us
    reduce_scatter x1, waiting for transfers between devices, body(): lax.psum_scatter(second_down_grad, ('item', 'lat', 'pix'), scatter_dimens...  152 us
    reduce_scatter x1, waiting for transfers between devices, body(): lax.psum_scatter(cross_out_grad, ('item', 'lat', 'pix'), scatter_dimensio...  151 us
    reduce_scatter x1, waiting for transfers between devices, body(): lax.psum_scatter(query_grad, ('item', 'lat', 'pix'), scatter_dimension=0,...  151 us
    reduce_scatter x1, waiting for transfers between devices, body(): lax.psum_scatter(first_down_grad, ('item', 'lat', 'pix'), scatter_dimensi...  150 us
    reduce_scatter x1, waiting for transfers between devices, body(): lax.psum_scatter(first_up_grad, ('item', 'lat', 'pix'), scatter_dimension...  150 us
    reduce_scatter x1, waiting for transfers between devices, body(): lax.psum_scatter(self_out_grad, ('item', 'lat', 'pix'), scatter_dimension...  150 us
  transfers between devices with their start and end apart: 15, of which 14 were waited for; matrix products, arithmetic and copies ran while one was open for 9% of the time, Pallas kernels for 0%

profile of v1, /device:TPU:0, one launch (start us, length us, event | category | flops | bytes accessed | tf_op | source)
XLA Modules:
  0.0 2264.6 jit_solution(4769851918985535743)
XLA Ops:
  14.7 5.0 convert_reduce_fusion
  22.3 20.9 convolution_convert_fusion.2
  43.2 20.6 convolution_convert_fusion.1
  67.1 18.0 fusion
  85.1 18.5 convolution_convert_fusion.5
  103.7 33.0 %psum.56 = bf16[4,512]{1,0:T(4,128)(2,1)S(1)} all-reduce(bf16[4,512]{1,0:T(4,128)(2,1)S(1)} %get-tuple-element.116), channel_id=1, replica_groups=mesh['item'=2,'lat'=4,'pix'=4] {'lat','pix'}, use_global_device_ids=true, to_apply=%region_6.7 | all-reduce | flops 2048 | bytes 8192 | tf_op jit(solution)/shard_map/psum | solution.py:127
  136.7 314.1 %all-gather.13.cloned.1.call-done = bf16[64,512,1024]{2,1,0:T(8,128)(2,1)} async-done(((bf16[4,512,1024]{2,1,0:T(8,128)(2,1)}), bf16[64,512,1024]{2,1,0:T(8,128)(2,1)}) %all-gather.13.cloned.1.call-update) | async-done | bytes 67108880 | tf_op jit(solution)/shard_map/all_gather | solution.py:124
  450.7 23.8 %reduce_sum.277 = bf16[4,512,1024]{2,1,0:T(8,128)(2,1)} reduce(bf16[16,4,512,1024]{3,2,1,0:T(8,128)(2,1)} %bitcast.4, bf16[]{:T(256)} %constant.77.clone.1), dimensions={0}, to_apply=%region_4.5 | reduce | flops 31457280 | bytes 71303168 | tf_op jit(solution)/shard_map/reduce_sum | solution.py:124
  479.7 3.9 convolution_convert_fusion.3
  489.1 71.0 %all-gather.9.cloned.1.call-done = bf16[4,512,2048]{2,0,1:T(4,128)(2,1)} async-done(((bf16[4,32,2048]{2,0,1:T(4,128)(2,1)}), bf16[4,512,2048]{2,0,1:T(4,128)(2,1)}) %all-gather.9.cloned.1.call-update) | async-done | bytes 8388624 | tf_op jit(solution)/shard_map/all_gather | solution.py:143
  560.1 8.5 fusion.91
  568.6 7.5 copy.107
  576.1 4.4 fusion.94
  580.5 7.5 copy.106
  588.0 4.5 fusion.95
  597.7 4.2 convolution_convert_fusion.4
  603.0 4.2 multiply_convert_fusion.3
  607.2 6.3 copy.93
  613.4 6.3 copy.94
  619.8 8.2 pad_maximum_fusion
  628.2 3.7 fusion.22
  632.0 98.1 %reduce-scatter.11.cloned.1.call-done = bf16[4,32,2048]{2,1,0:T(8,128)(2,1)} async-done(((bf16[4,512,2048]{2,1,0:T(8,128)(2,1)}), bf16[4,32,2048]{2,1,0:T(8,128)(2,1)}) %reduce-scatter.11.cloned.1.call-update) | async-done | bytes 524304 | tf_op jit(solution)/shard_map/reduce_scatter | solution.py:197
  730.2 5.4 multiply_reduce_fusion.2
  742.3 31.2 %all-gather.1 = bf16[16,32,4]{1,2,0:T(4,128)(2,1)S(1)} all-gather(bf16[1,32,4]{1,2,0:T(4,128)(2,1)S(1)} %fusion.74), channel_id=1, replica_groups=mesh['item'=2,'lat'=4,'pix'=4] {'lat','pix'}, dimensions={0}, use_global_device_ids=true | all-gather | bytes 4352 | tf_op jit(solution)/shard_map/all_gather | solution.py:220
  773.6 19.0 all-gather.11.cloned.1.call-done
  792.6 16.2 multiply_convert_fusion.1
  812.0 13.7 multiply_convert_fusion.2
  845.2 13.2 convolution_convert_fusion
  858.4 5.7 copy-done.65
  864.1 11.7 convolution_bitcast_fusion.1
  875.7 16.0 multiply_convert_fusion
  891.8 16.4 convolution_bitcast_fusion.2
  908.2 6.4 fusion.47
  915.6 3.7 convolution_bitcast_fusion
  922.2 19.6 fusion.25
  941.9 17.8 fusion.13
  959.7 6.5 fusion.12
  966.2 5.3 copy.98
  972.5 40.7 %all-reduce = (f32[1024]{0:T(1024)}, f32[261]{0:T(512)}, f32[1024]{0:T(1024)}, f32[1024]{0:T(1024)}, f32[1024]{0:T(1024)}) all-reduce(f32[1024]{0:T(1024)S(1)} %get-tuple-element.99, f32[261]{0:T(512)S(1)} %get-tuple-element.90, f32[1024]{0:T(1024)S(1)} %get-tuple-element.97, ...), channel_id=1, replica_groups=mesh['item'=2,'lat'=4,'pix'=4] {'item','lat','pix'}, use_global_device_ids=true, to_apply=%region_39.40 | all-reduce | flops 4357 | bytes 34856 | tf_op jit(solution)/shard_map/psum | solution.py:290
  1014.3 34.0 %reduce-scatter.27.cloned.1.call-done = f32[32,1024]{1,0:T(8,128)} async-done(((f32[1024,1024]{1,0:T(8,128)}), f32[32,1024]{1,0:T(8,128)}) %reduce-scatter.27.cloned.1.call-update) | async-done | bytes 131088 | tf_op jit(solution)/shard_map/reduce_scatter | solution.py:279
  1048.3 150.0 %reduce-scatter.25.cloned.1.call-done = f32[32,1024]{1,0:T(8,128)} async-done(((f32[1024,1024]{1,0:T(8,128)}), f32[32,1024]{1,0:T(8,128)}) %reduce-scatter.25.cloned.1.call-update) | async-done | bytes 131088 | tf_op jit(solution)/shard_map/reduce_scatter | solution.py:278
  1198.3 151.6 %reduce-scatter.29.cloned.1.call-done = f32[32,1024]{1,0:T(8,128)} async-done(((f32[1024,1024]{1,0:T(8,128)}), f32[32,1024]{1,0:T(8,128)}) %reduce-scatter.29.cloned.1.call-update) | async-done | bytes 131088 | tf_op jit(solution)/shard_map/reduce_scatter | solution.py:280
  1349.9 150.2 %reduce-scatter.19.cloned.1.call-done = f32[32,1024]{1,0:T(8,128)} async-done(((f32[1024,1024]{1,0:T(8,128)}), f32[32,1024]{1,0:T(8,128)}) %reduce-scatter.19.cloned.1.call-update) | async-done | bytes 131088 | tf_op jit(solution)/shard_map/reduce_scatter | solution.py:275
  1500.1 151.4 %reduce-scatter.17.cloned.1.call-done = f32[32,1024]{1,0:T(8,128)} async-done(((f32[1024,1024]{1,0:T(8,128)}), f32[32,1024]{1,0:T(8,128)}) %reduce-scatter.17.cloned.1.call-update) | async-done | bytes 131088 | tf_op jit(solution)/shard_map/reduce_scatter | solution.py:274
  1651.5 150.3 %reduce-scatter.21.cloned.1.call-done = f32[32,1024]{1,0:T(8,128)} async-done(((f32[1024,1024]{1,0:T(8,128)}), f32[32,1024]{1,0:T(8,128)}) %reduce-scatter.21.cloned.1.call-update) | async-done | bytes 131088 | tf_op jit(solution)/shard_map/reduce_scatter | solution.py:276
  1801.8 140.0 %all-reduce.4.cloned.1.call-done = (f32[261,1024]{1,0:T(8,128)}, f32[261,1024]{1,0:T(8,128)}) async-done(((f32[261,1024]{1,0:T(8,128)}, f32[261,1024]{1,0:T(8,128)}), (f32[261,1024]{1,0:T(8,128)}, f32[261,1024]{1,0:T(8,128)})) %all-reduce.4.cloned.1.call-update) | async-done | bytes 2138128 | tf_op jit(solution)/shard_map/psum | solution.py:290
  1941.8 160.5 %reduce-scatter.23.cloned.1.call-done = f32[32,3072]{1,0:T(8,128)} async-done(((f32[1024,3072]{1,0:T(8,128)}), f32[32,3072]{1,0:T(8,128)}) %reduce-scatter.23.cloned.1.call-update) | async-done | bytes 393232 | tf_op jit(solution)/shard_map/reduce_scatter | solution.py:277
  2102.4 150.6 %reduce-scatter.15.cloned.1.call-done = f32[32,1024]{1,0:T(8,128)} async-done(((f32[1024,1024]{1,0:T(8,128)}), f32[32,1024]{1,0:T(8,128)}) %reduce-scatter.15.cloned.1.call-update) | async-done | bytes 131088 | tf_op jit(solution)/shard_map/reduce_scatter | solution.py:273
  (242 shorter events, 70.0 us)
Async XLA Ops:
  7.2 586.3 %copy-start = (bf16[1024,1024]{1,0:T(8,128)(2,1)S(1)}, bf16[1024,1024]{1,0:T(8,128)(2,1)}, u32[]{:S(2)}) copy-start(bf16[1024,1024]{1,0:T(8,128)(2,1)} %param.35) | copy-start | bytes 6291460
  7.2 59.9 %all-gather.7.cloned.1.call-start = ((), (), s32[]{:S(2)}) async-start(), calls=%async_computation.10 | async-start | bytes 4456448 | tf_op jit(solution)/shard_map/all_gather | solution.py:104
  8.5 13.7 copy-start.48
  9.7 12.4 copy-start.54
  9.7 12.4 copy-start.52
  9.8 12.4 copy-start.56
  13.8 437.0 %all-gather.13.cloned.1.call-start = ((), (), s32[]{:S(2)}) async-start(), calls=%async_computation.23 | async-start | bytes 71303168 | tf_op jit(solution)/shard_map/all_gather | solution.py:124
  13.8 5.9 copy-start.3
  14.7 7.5 copy-start.58
  14.7 7.5 copy-start.60
  19.8 23.4 %copy-start.41 = (f32[4,2048]{1,0:T(4,128)}, f32[4,2048]{1,0:T(4,128)S(1)}, u32[]{:S(2)}) copy-start(f32[4,2048]{1,0:T(4,128)S(1)} %broadcast_multiply_fusion.2) | copy-start | bytes 98308
  22.2 20.9 copy-start.44
  22.3 20.9 copy-start.62
  103.6 456.5 %all-gather.9.cloned.1.call-start = ((), (), s32[]{:S(2)}) async-start(), calls=%async_computation.11 | async-start | bytes 8912896 | tf_op jit(solution)/shard_map/all_gather | solution.py:143
  450.7 25.1 %copy-start.15 = (bf16[4,32,1024]{2,1,0:T(8,128)(2,1)S(1)}, bf16[4,32,1024]{2,1,0:T(8,128)(2,1)}, u32[]{:S(2)}) copy-start(bf16[4,32,1024]{2,1,0:T(8,128)(2,1)} %param.19) | copy-start | bytes 786436
  450.7 27.6 %copy-start.46 = (f32[1024]{0:T(1024)S(1)}, f32[1024]{0:T(1024)}, u32[]{:S(2)}) copy-start(f32[1024]{0:T(1024)} %param.28) | copy-start | bytes 12292
  479.7 6.1 copy-start.25
  485.8 244.4 %reduce-scatter.11.cloned.1.call-start = ((), (), s32[]{:S(2)}) async-start(), calls=%async_computation.12 | async-start | bytes 8912896 | tf_op jit(solution)/shard_map/reduce_scatter | solution.py:197
  588.0 5.5 copy-start.40
  588.0 5.5 copy-start.47
  627.9 164.7 %all-gather.11.cloned.1.call-start = ((), (), s32[]{:S(2)}) async-start(), calls=%async_computation.13 | async-start | bytes 4456448 | tf_op jit(solution)/shard_map/all_gather | solution.py:219
  632.0 98.1 %copy-start.37 = (bf16[16,8,8,128]{3,1,2,0:T(8,128)(2,1)}, bf16[16,8,8,128]{3,1,2,0:T(8,128)(2,1)S(1)}, u32[]{:S(2)}) copy-start(bf16[16,8,8,128]{3,1,2,0:T(8,128)(2,1)S(1)} %copy.148) | copy-start | bytes 786436
  730.2 6.9 copy-start.21
  730.2 6.9 copy-start.30
  739.4 100.2 %copy-start.7 = (f32[128,1024]{1,0:T(8,128)}, f32[128,1024]{1,0:T(8,128)S(1)}, u32[]{:S(2)}) copy-start(f32[128,1024]{1,0:T(8,128)S(1)} %multiply_add_fusion) | copy-start | bytes 1572868
  742.2 172.6 %reduce-scatter.13.cloned.1.call-start = ((), (), s32[]{:S(2)}) async-start(), calls=%async_computation.14 | async-start | bytes 4456448 | tf_op jit(solution)/shard_map/reduce_scatter | solution.py:234
  825.7 222.5 %reduce-scatter.27.cloned.1.call-start = ((), (), s32[]{:S(2)}) async-start(), calls=%async_computation.21 | async-start | bytes 4325376 | tf_op jit(solution)/shard_map/reduce_scatter | solution.py:279
  829.6 368.7 %reduce-scatter.25.cloned.1.call-start = ((), (), s32[]{:S(2)}) async-start(), calls=%async_computation.20 | async-start | bytes 4325376 | tf_op jit(solution)/shard_map/reduce_scatter | solution.py:278
  832.8 517.1 %reduce-scatter.29.cloned.1.call-start = ((), (), s32[]{:S(2)}) async-start(), calls=%async_computation.22 | async-start | bytes 4325376 | tf_op jit(solution)/shard_map/reduce_scatter | solution.py:280
  836.6 663.5 %reduce-scatter.19.cloned.1.call-start = ((), (), s32[]{:S(2)}) async-start(), calls=%async_computation.17 | async-start | bytes 4325376 | tf_op jit(solution)/shard_map/reduce_scatter | solution.py:275
  839.5 812.0 %reduce-scatter.17.cloned.1.call-start = ((), (), s32[]{:S(2)}) async-start(), calls=%async_computation.16 | async-start | bytes 4325376 | tf_op jit(solution)/shard_map/reduce_scatter | solution.py:274
  842.3 959.6 %reduce-scatter.21.cloned.1.call-start = ((), (), s32[]{:S(2)}) async-start(), calls=%async_computation.18 | async-start | bytes 4325376 | tf_op jit(solution)/shard_map/reduce_scatter | solution.py:276
  845.1 19.0 copy-start.42
  845.1 19.0 copy-start.45
  845.1 19.0 copy-start.59
  845.1 1096.7 %all-reduce.4.cloned.1.call-start = ((), (), s32[]{:S(2)}) async-start(), calls=%async_computation.24 | async-start | bytes 4325376 | tf_op jit(solution)/shard_map/psum | solution.py:290
  858.4 5.7 copy-start.65
  891.8 16.4 copy-start.38
  891.8 16.5 copy-start.39
  908.2 1194.2 %reduce-scatter.23.cloned.1.call-start = ((), (), s32[]{:S(2)}) async-start(), calls=%async_computation.19 | async-start | bytes 12976128 | tf_op jit(solution)/shard_map/reduce_scatter | solution.py:277
  914.7 1338.3 %reduce-scatter.15.cloned.1.call-start = ((), (), s32[]{:S(2)}) async-start(), calls=%async_computation.15 | async-start | bytes 4325376 | tf_op jit(solution)/shard_map/reduce_scatter | solution.py:273
  919.3 22.5 slice-start
  922.2 19.6 slice-start.1
  922.2 19.6 copy-start.63
  966.1 5.4 copy-start.28
  966.2 6.4 copy-start.51
  966.2 47.1 %copy-start.8 = (f32[128,1024]{1,0:T(8,128)S(1)}, f32[128,1024]{1,0:T(8,128)}, u32[]{:S(2)}) copy-start(f32[128,1024]{1,0:T(8,128)} %copy-done.7) | copy-start | bytes 1572868
  971.6 1286.1 %copy-start.1 = (bf16[1024,1024]{1,0:T(8,128)(2,1)S(1)}, bf16[1024,1024]{1,0:T(8,128)(2,1)}, u32[]{:S(2)}) copy-start(bf16[1024,1024]{1,0:T(8,128)(2,1)} %param.35) | copy-start | bytes 6291460
  (36 other events, 99.4 us)
Sparse Core Ops, SparseCore 0:
  13.9 53.1 all-gather.6
  103.7 346.9 all-gather.12
  485.9 74.1 all-gather.8
  628.1 102.0 reduce-scatter.10
  742.3 50.2 all-gather.10
  825.8 71.2 reduce-scatter.12
  900.0 148.2 reduce-scatter.26
  1051.1 147.1 reduce-scatter.24
  1201.2 148.6 reduce-scatter.28
  1352.6 147.4 reduce-scatter.18
  1503.0 148.5 reduce-scatter.16
  1654.2 147.5 reduce-scatter.20
  1808.2 133.6 all-reduce.3
  1948.3 154.0 reduce-scatter.22
  2105.1 147.8 reduce-scatter.14
